TPU v7x, 128 devices: a whole 4x4x4 slice. The times are simulated.
128 devices in a mesh: dp: 2 (over y_lo), ctx: 64 (over x, y_hi, z, core).
Axes of the slice: x: 4, y: 4 (y_hi: 2, y_lo: 2; y = y_hi * 2 + y_lo), z: 4, core: 2. Of those that a mesh axis runs over, the one named last changes fastest.
Arguments:
- tokens: bfloat16 [2, 24576, 2560], P('dp', 'ctx'), may hold values from -32 to 32
- qkv_weight: bfloat16 [2560, 3840], P(None, 'dp'), may hold values from -8 to 8
- out_weight: bfloat16 [1280, 2560], P(None, 'dp'), may hold values from -3.5 to 3.5
- offsets: int32 [4, 10], replicated, may hold values from 0 to 7, as said below
Outputs:
- mixed: bfloat16 [2, 24576, 2560], P('dp', 'ctx')
Inputs may be any that keep to these rules, and one draw needn't show every extreme that they name: offsets[j, h] is at most 2 ** j - 1 for level j.
All inputs are finite; a program needn't handle non-finite values.
Results may differ from a plain program's by a relative error of at most 0.0083.
Values may be sent and summed in bfloat16 or wider, within the bound.
No kernel may reach another device: no remote copies, remote signals or barrier semaphores. Data moves between devices by JAX's collectives and lax.ppermute only.
A program may use at most 192 MiB of HBM per device.

v0:
```python
import jax
import jax.numpy as jnp
from jax import lax
from jax.sharding import PartitionSpec as P


def from_partner(block, axis, stride):
    count = lax.axis_size(axis)
    route = []
    for low in range(count):
        high = low | 1 << stride
        if high != low and high < count:
            route += [(low, high), (high, low)]
    return lax.ppermute(block, axis, route)


def pick_table(offset_row, dilation):
    return jnp.arange(dilation, dtype=jnp.int32)[:, None] == offset_row[None, :]


def select_rows(values_in, chosen, dilation):
    array_shape = values_in.shape
    grouped = values_in.reshape((array_shape[0] // dilation, dilation) + array_shape[1:])
    middle_dims = len(array_shape) - 3
    table = chosen.reshape((1, dilation) + (1,) * middle_dims + (chosen.shape[1], 1))
    return jnp.sum(jnp.where(table, grouped, jnp.zeros((), grouped.dtype)), axis=1)


def attend(queries, key_rows, value_rows, score_scale):
    scores = (
        jnp.einsum("qhd,khd->hqk", queries, key_rows, preferred_element_type=jnp.float32)
        * score_scale
    )
    row_max = jnp.max(scores, axis=2, keepdims=True)
    expo = jnp.exp(scores - row_max)
    row_total = jnp.sum(expo, axis=2)
    blended = jnp.einsum(
        "hqk,khd->qhd", expo.astype(jnp.bfloat16), value_rows, preferred_element_type=jnp.float32
    )
    return (blended / row_total.T[:, :, None], (row_max[:, :, 0] + jnp.log(row_total)).T)


def local(tokens, qkv_weight, out_weight, offsets):
    tok_rows = tokens.shape[1]
    level_count = offsets.shape[0]
    head_count = offsets.shape[1]
    inner_width = out_weight.shape[0]
    head_size = inner_width // head_count
    token_flat = tokens.reshape(tok_rows, tokens.shape[2])
    projected = jnp.dot(
        token_flat,
        lax.all_gather(qkv_weight, "dp", axis=1, tiled=True),
        preferred_element_type=jnp.float32,
    ).astype(jnp.bfloat16)
    all_query = projected[:, :inner_width].reshape(tok_rows, head_count, head_size)
    keyval = projected[:, inner_width:].reshape(tok_rows, 2, head_count, head_size)
    pick_tables = [pick_table(offsets[degree], 2**degree) for degree in range(level_count)]
    queries = [
        select_rows(all_query, pick_tables[degree], 2**degree) for degree in range(level_count)
    ]
    pieces = [
        select_rows(keyval, pick_tables[degree], 2**degree).reshape(
            tok_rows // 2**degree, 2, inner_width
        )
        for degree in range(level_count)
    ]
    bit_order = list(range(level_count))
    collected = []
    for degree in range(level_count):
        gathered = pieces[degree]
        for which_bit in bit_order:
            if which_bit <= degree:
                partner = from_partner(gathered, "ctx", which_bit)
                gathered = jnp.concatenate([gathered, partner], axis=0)
        collected.append(gathered)
    score_scale = head_size ** (-0.5)
    for degree in range(level_count):
        key_rows = collected[degree][:, 0].reshape(-1, head_count, head_size)
        value_rows = collected[degree][:, 1].reshape(-1, head_count, head_size)
        blended, row_lse = attend(queries[degree], key_rows, value_rows, score_scale)
        chosen = pick_tables[degree][None, :, :]
        level_out = jnp.where(chosen[..., None], blended[:, None], 0.0).reshape(
            tok_rows, head_count, head_size
        )
        level_lse = jnp.where(chosen, row_lse[:, None], -jnp.inf).reshape(tok_rows, head_count)
        if degree == 0:
            weighted = level_out
            totals = jnp.ones_like(level_lse)
            running = level_lse
        else:
            newest = jnp.maximum(running, level_lse)
            former = jnp.exp(running - newest)
            fresh = jnp.exp(level_lse - newest)
            weighted = weighted * former[..., None] + fresh[..., None] * level_out
            totals = totals * former + fresh
            running = newest
    attended = (weighted / totals[..., None]).astype(jnp.bfloat16).reshape(tok_rows, inner_width)
    mixed = jnp.dot(
        attended,
        lax.all_gather(out_weight, "dp", axis=1, tiled=True),
        preferred_element_type=jnp.float32,
    ).astype(jnp.bfloat16)
    return mixed.reshape(1, tok_rows, mixed.shape[1])


def solution(mesh):
    in_specs = (P("dp", "ctx", None), P(None, "dp"), P(None, "dp"), P())
    out_specs = P("dp", "ctx", None)
    return jax.shard_map(local, mesh=mesh, in_specs=in_specs, out_specs=out_specs, check_vma=False)
```

profile of v0, /device:TPU:0, one launch (start us, length us, event | category | flops | bytes accessed | tf_op | source)
XLA Modules:
  0.0 501.0 jit_solution(6811902256076072925)
XLA Ops:
  8.9 238.1 %all-gather.3.cloned.1.call-done = bf16[2560,3840]{1,0:T(8,128)(2,1)} async-done(((bf16[2560,1920]{1,0:T(8,128)(2,1)}), bf16[2560,3840]{1,0:T(8,128)(2,1)}) %all-gather.3.cloned.1.call-update) | async-done | bytes 19660816 | tf_op jit(solution)/shard_map/all_gather | solution.py:52
  247.0 12.3 %convolution_convert_fusion = bf16[384,3840]{1,0:T(8,128)(2,1)S(1)} fusion(bf16[2560,3840]{1,0:T(8,128)(2,1)} %all-gather.3.cloned.1.call-done, bf16[1,384,2560]{2,1,0:T(8,128)(2,1)S(1)} %copy-done), kind=kOutput, calls=%fused_computation.8 | convolution fusion | flops 7551221760 | bytes 24576000 | tf_op jit(solution)/shard_map/dot_general | solution.py:50
  259.5 1.5 copy-done.14
  261.0 2.7 reshape_reshape.27
  263.8 2.7 reshape_reshape.29
  266.5 2.9 fusion.41
  269.4 2.3 copy.120
  271.6 1.5 reshape_reshape.28
  273.1 1.3 copy.71
  274.4 4.9 select_reduce_fusion.1
  279.4 2.0 copy.74
  281.4 1.4 copy.75
  282.8 4.2 select_reduce_fusion
  286.9 2.6 copy.87
  289.5 2.1 copy.88
  291.6 0.9 collective-permute-start.3
  292.5 2.1 select_reduce_fusion.2
  294.6 1.1 reshape.386
  296.5 3.2 broadcast_select_fusion
  299.7 1.5 reshape_reshape.26
  301.2 3.4 select_reduce_fusion.4
  305.2 0.9 pad_maximum_fusion.8
  306.0 1.6 collective-permute-start.7
  307.6 1.4 select_reduce_fusion.3
  309.0 1.4 copy.93
  310.4 1.6 pad_maximum_fusion.6
  312.0 2.3 copy.90
  314.8 5.5 %collective-permute-done.7 = bf16[96,2,1280]{2,0,1:T(8,128)(2,1)S(1)} collective-permute-done((bf16[96,2,1280]{2,0,1:T(8,128)(2,1)}, bf16[96,2,1280]{2,0,1:T(8,128)(2,1)S(1)}, u32[]{:S(2)}, u32[]{:S(2)}) %collective-permute-start.7) | collective-permute-done | bytes 491552 | tf_op jit(solution)/shard_map/ppermute | solution.py:14
  320.3 2.2 pad_maximum_fusion.7
  322.5 3.2 collective-permute-start.8
  327.2 1.5 copy.77
  328.7 2.0 pad_maximum_fusion.3
  331.4 10.1 %collective-permute-done.4 = bf16[192,2,1280]{2,0,1:T(8,128)(2,1)} collective-permute-done((bf16[192,2,1280]{2,0,1:T(8,128)(2,1)}, bf16[192,2,1280]{2,0,1:T(8,128)(2,1)}, u32[]{:S(2)}, u32[]{:S(2)}) %collective-permute-start.4) | collective-permute-done | bytes 983072 | tf_op jit(solution)/shard_map/ppermute | solution.py:14
  341.5 1.5 copy.94
  343.1 3.5 pad_maximum_fusion.4
  346.6 3.2 collective-permute-start.5
  349.7 15.2 %collective-permute-done.8 = bf16[192,2,1280]{2,0,1:T(8,128)(2,1)} collective-permute-done((bf16[192,2,1280]{2,0,1:T(8,128)(2,1)}, bf16[192,2,1280]{2,0,1:T(8,128)(2,1)}, u32[]{:S(2)}, u32[]{:S(2)}) %collective-permute-start.8) | collective-permute-done | bytes 983072 | tf_op jit(solution)/shard_map/ppermute | solution.py:14
  365.0 2.6 pad_maximum_fusion.5
  367.6 2.7 collective-permute-start.9
  370.3 2.3 constant_dynamic-update-slice_fusion.1
  372.5 3.5 pad_maximum_fusion.2
  376.0 1.9 multiply_reduce_fusion
  378.0 2.7 fusion
  380.7 1.6 copy-done.2
  382.3 22.4 %collective-permute-done.2 = bf16[384,2,1280]{0,2,1:T(8,128)(2,1)} collective-permute-done((bf16[384,2,1280]{0,2,1:T(8,128)(2,1)}, bf16[384,2,1280]{0,2,1:T(8,128)(2,1)}, u32[]{:S(2)}, u32[]{:S(2)}) %collective-permute-start.2) | collective-permute-done | bytes 1966112 | tf_op jit(solution)/shard_map/ppermute | solution.py:14
  404.7 2.7 pad_maximum_fusion
  408.5 1.0 multiply_reduce_fusion.1
  409.5 1.4 fusion.7
  410.9 1.6 fusion.45
  413.4 2.2 copy.141
  415.5 2.9 copy.86
  418.7 29.5 %collective-permute-done.5 = bf16[384,2,1280]{0,2,1:T(8,128)(2,1)} collective-permute-done((bf16[384,2,1280]{0,2,1:T(8,128)(2,1)}, bf16[384,2,1280]{0,2,1:T(8,128)(2,1)}, u32[]{:S(2)}, u32[]{:S(2)}) %collective-permute-start.5) | collective-permute-done | bytes 1966112 | tf_op jit(solution)/shard_map/ppermute | solution.py:14
  448.2 3.5 pad_maximum_fusion.1
  454.1 1.4 fusion.38
  456.0 0.9 copy.140
  456.9 1.8 copy.103
  459.0 3.0 constant_dynamic-update-slice_fusion
  462.0 4.4 fusion.67
  466.4 2.7 copy.105
  469.1 4.1 copy.108
  475.8 1.8 copy.111
  478.0 7.8 %fusion.21 = f32[384,10,128]{0,2,1:T(8,128)S(1)} fusion(bf16[768,10,128]{0,2,1:T(8,128)(2,1)} %bitcast.162, f32[10,384,768]{2,1,0:T(8,128)} %copy-done.2, f32[10,384]{1,0:T(8,128)S(1)} %get-tuple-element.25, f32[384,10]{0,1:T(8,128)S(1)} %get-tuple-element.11, f32[384,10]{0,1:T(8,128)S(1)} %bitcast.168, pred[10]{0:T(512)(128)(4,1)S(1)} %compare_bitcast_fusion), kind=kOutput, calls=%fused_computation.46 | convolution fusion | flops 765296640 | bytes 15774730 | tf_op jit(solution)/shard_map/hqk,khd->qhd/dot_general | solution.py:37
  485.9 1.0 fusion.16
  486.9 7.0 %fusion.8 = bf16[1,384,2560]{2,1,0:T(8,128)(2,1)} fusion(bf16[384,1280]{0,1:T(8,128)(2,1)S(1)} %fusion.16, bf16[1280,2560]{1,0:T(8,128)(2,1)} %all-gather.5.cloned.1.call-done), kind=kOutput, calls=%fused_computation.17 | convolution fusion | flops 2517565440 | bytes 9502720 | tf_op jit(solution)/shard_map/dot_general | solution.py:98
  (116 shorter events, 14.9 us)
Async XLA Ops:
  6.5 240.4 %copy-start = (bf16[1,384,2560]{2,1,0:T(8,128)(2,1)S(1)}, bf16[1,384,2560]{2,1,0:T(8,128)(2,1)}, u32[]{:S(2)}) copy-start(bf16[1,384,2560]{2,1,0:T(8,128)(2,1)} %param.4) | copy-start | bytes 5898244
  6.5 240.4 %all-gather.3.cloned.1.call-start = ((), (), s32[]{:S(2)}) async-start(), calls=%async_computation | async-start | bytes 29491200 | tf_op jit(solution)/shard_map/all_gather | solution.py:52
  7.3 0.8 copy-start.29
  7.3 479.6 %all-gather.5.cloned.1.call-start = ((), (), s32[]{:S(2)}) async-start(), calls=%async_computation.1 | async-start | bytes 9830400 | tf_op jit(solution)/shard_map/all_gather | solution.py:100
  8.1 266.4 %copy-start.27 = (pred[2,10]{1,0:T(4,128)(4,1)}, pred[2,10]{1,0:T(4,128)(4,1)S(1)}, u32[]{:S(2)}) copy-start(pred[2,10]{1,0:T(4,128)(4,1)S(1)} %iota_compare_fusion.2) | copy-start | bytes 64
  8.1 274.7 %copy-start.25 = (pred[4,10]{1,0:T(4,128)(4,1)}, pred[4,10]{1,0:T(4,128)(4,1)S(1)}, u32[]{:S(2)}) copy-start(pred[4,10]{1,0:T(4,128)(4,1)S(1)} %iota_compare_fusion.1) | copy-start | bytes 124
  259.3 1.6 copy-start.14
  261.0 12.1 %copy-start.4 = (bf16[384,1280]{1,0:T(8,128)(2,1)}, bf16[384,1280]{1,0:T(8,128)(2,1)S(1)}, u32[]{:S(2)}) copy-start(bf16[384,1280]{1,0:T(8,128)(2,1)S(1)} %slice.68) | copy-start | bytes 2949124
  282.8 44.4 %collective-permute-start.1 = (bf16[192,2,1280]{2,0,1:T(8,128)(2,1)}, bf16[192,2,1280]{2,0,1:T(8,128)(2,1)}, u32[]{:S(2)}, u32[]{:S(2)}) collective-permute-start(bf16[192,2,1280]{2,0,1:T(8,128)(2,1)} %copy.75), channel_id=1, source_target_pairs={{0,1},{1,0},{2,3},{3,2},{4,5},{5,4},{6,7},{7,6},{8,9},{9,8},{10,11... | collective-permute-start | bytes 2949128 | tf_op jit(solution)/shard_map/ppermute | solution.py:14
  291.6 17.4 %collective-permute-start.3 = (bf16[96,2,1280]{2,0,1:T(8,128)(2,1)}, bf16[96,2,1280]{2,0,1:T(8,128)(2,1)}, u32[]{:S(2)}, u32[]{:S(2)}) collective-permute-start(bf16[96,2,1280]{2,0,1:T(8,128)(2,1)} %copy.88), channel_id=1, source_target_pairs={{0,1},{1,0},{2,3},{3,2},{4,5},{5,4},{6,7},{7,6},{8,9},{9,8},{10,11... | collective-permute-start | bytes 1474568 | tf_op jit(solution)/shard_map/ppermute | solution.py:14
  296.5 8.7 %collective-permute-start.6 = (bf16[48,2,1280]{2,0,1:T(8,128)(2,1)S(1)}, bf16[48,2,1280]{2,0,1:T(8,128)(2,1)S(1)}, u32[]{:S(2)}, u32[]{:S(2)}) collective-permute-start(bf16[48,2,1280]{2,0,1:T(8,128)(2,1)S(1)} %get-tuple-element.20), channel_id=1, source_target_pairs={{0,1},{1,0},{2,3},{3,2},{4,5},{5,4},{6,7},{7,6},{8,9},{9,8},{10,11... | collective-permute-start | bytes 737288 | tf_op jit(solution)/shard_map/ppermute | solution.py:14
  296.5 3.2 copy-start.5
  299.7 1.5 copy-start.28
  301.2 6.3 %copy-start.13 = (bf16[96,4,10,128]{3,2,1,0:T(8,128)(2,1)S(1)}, bf16[96,4,10,128]{3,2,1,0:T(8,128)(2,1)}, u32[]{:S(2)}) copy-start(bf16[96,4,10,128]{3,2,1,0:T(8,128)(2,1)} %reshape_reshape.28) | copy-start | bytes 2949124
  301.2 6.3 %copy-start.26 = (pred[4,10]{1,0:T(4,128)(4,1)S(1)}, pred[4,10]{1,0:T(4,128)(4,1)}, u32[]{:S(2)}) copy-start(pred[4,10]{1,0:T(4,128)(4,1)} %copy-done.25) | copy-start | bytes 124
  304.6 5.7 %copy-start.3 = (bf16[96,2,10,128]{0,3,2,1:T(8,128)(2,1)S(1)}, bf16[96,2,10,128]{0,3,2,1:T(8,128)(2,1)}, u32[]{:S(2)}) copy-start(bf16[96,2,10,128]{0,3,2,1:T(8,128)(2,1)} %copy.87) | copy-start | bytes 1474564
  304.7 67.9 %collective-permute-start = (bf16[384,2,1280]{0,2,1:T(8,128)(2,1)}, bf16[384,2,1280]{0,2,1:T(8,128)(2,1)}, u32[]{:S(2)}, u32[]{:S(2)}) collective-permute-start(bf16[384,2,1280]{0,2,1:T(8,128)(2,1)} %broadcast_select_fusion), channel_id=1, source_target_pairs={{0,1},{1,0},{2,3},{3,2},{4,5},{5,4},{6,7},{7,6},{8,9},{9,8},{10,11... | collective-permute-start | bytes 5898248 | tf_op jit(solution)/shard_map/ppermute | solution.py:14
  305.1 3.9 copy-start.18
  306.0 14.3 %collective-permute-start.7 = (bf16[96,2,1280]{2,0,1:T(8,128)(2,1)}, bf16[96,2,1280]{2,0,1:T(8,128)(2,1)S(1)}, u32[]{:S(2)}, u32[]{:S(2)}) collective-permute-start(bf16[96,2,1280]{2,0,1:T(8,128)(2,1)} %pad_maximum_fusion.8), channel_id=1, source_target_pairs={{0,2},{2,0},{1,3},{3,1},{4,6},{6,4},{5,7},{7,5},{8,10},{10,8},{9,1... | collective-permute-start | bytes 1474568 | tf_op jit(solution)/shard_map/ppermute | solution.py:14
  310.4 4.0 copy-start.8
  314.4 11.3 %copy-start.19 = (bf16[48,2,1280]{2,0,1:T(8,128)(2,1)S(1)}, bf16[48,2,1280]{2,0,1:T(8,128)(2,1)}, u32[]{:S(2)}) copy-start(bf16[48,2,1280]{2,0,1:T(8,128)(2,1)} %copy-done.18) | copy-start | bytes 737284
  314.4 27.1 %collective-permute-start.4 = (bf16[192,2,1280]{2,0,1:T(8,128)(2,1)}, bf16[192,2,1280]{2,0,1:T(8,128)(2,1)}, u32[]{:S(2)}, u32[]{:S(2)}) collective-permute-start(bf16[192,2,1280]{2,0,1:T(8,128)(2,1)} %copy.90), channel_id=1, source_target_pairs={{0,2},{2,0},{1,3},{3,1},{4,6},{6,4},{5,7},{7,5},{8,10},{10,8},{9,1... | collective-permute-start | bytes 2949128 | tf_op jit(solution)/shard_map/ppermute | solution.py:14
  320.3 6.9 %copy-start.15 = (bf16[96,2,1280]{2,0,1:T(8,128)(2,1)}, bf16[96,2,1280]{2,0,1:T(8,128)(2,1)S(1)}, u32[]{:S(2)}) copy-start(bf16[96,2,1280]{2,0,1:T(8,128)(2,1)S(1)} %collective-permute-done.7) | copy-start | bytes 1474564
  322.5 42.5 %collective-permute-start.8 = (bf16[192,2,1280]{2,0,1:T(8,128)(2,1)}, bf16[192,2,1280]{2,0,1:T(8,128)(2,1)}, u32[]{:S(2)}, u32[]{:S(2)}) collective-permute-start(bf16[192,2,1280]{2,0,1:T(8,128)(2,1)} %pad_maximum_fusion.7), channel_id=1, source_target_pairs={{0,4},{4,0},{1,5},{5,1},{2,6},{6,2},{3,7},{7,3},{8,12},{12,8},{9,1... | collective-permute-start | bytes 2949128 | tf_op jit(solution)/shard_map/ppermute | solution.py:14
  328.7 2.0 copy-start.6
  330.8 73.9 %collective-permute-start.2 = (bf16[384,2,1280]{0,2,1:T(8,128)(2,1)}, bf16[384,2,1280]{0,2,1:T(8,128)(2,1)}, u32[]{:S(2)}, u32[]{:S(2)}) collective-permute-start(bf16[384,2,1280]{0,2,1:T(8,128)(2,1)} %pad_maximum_fusion.3), channel_id=1, source_target_pairs={{0,2},{2,0},{1,3},{3,1},{4,6},{6,4},{5,7},{7,5},{8,10},{10,8},{9,1... | collective-permute-start | bytes 5898248 | tf_op jit(solution)/shard_map/ppermute | solution.py:14
  343.0 21.9 %copy-start.16 = (bf16[96,2,1280]{2,0,1:T(8,128)(2,1)S(1)}, bf16[96,2,1280]{2,0,1:T(8,128)(2,1)}, u32[]{:S(2)}) copy-start(bf16[96,2,1280]{2,0,1:T(8,128)(2,1)} %copy-done.15) | copy-start | bytes 1474564
  343.0 21.9 %copy-start.20 = (bf16[48,2,1280]{2,0,1:T(8,128)(2,1)S(1)}, bf16[48,2,1280]{2,0,1:T(8,128)(2,1)}, u32[]{:S(2)}) copy-start(bf16[48,2,1280]{2,0,1:T(8,128)(2,1)} %copy-done.18) | copy-start | bytes 737284
  346.6 101.6 %collective-permute-start.5 = (bf16[384,2,1280]{0,2,1:T(8,128)(2,1)}, bf16[384,2,1280]{0,2,1:T(8,128)(2,1)}, u32[]{:S(2)}, u32[]{:S(2)}) collective-permute-start(bf16[384,2,1280]{0,2,1:T(8,128)(2,1)} %pad_maximum_fusion.4), channel_id=1, source_target_pairs={{0,4},{4,0},{1,5},{5,1},{2,6},{6,2},{3,7},{7,3},{8,12},{12,8},{9,1... | collective-permute-start | bytes 5898248 | tf_op jit(solution)/shard_map/ppermute | solution.py:14
  367.6 91.4 %collective-permute-start.9 = (bf16[384,2,1280]{2,0,1:T(8,128)(2,1)}, bf16[384,2,1280]{2,0,1:T(8,128)(2,1)}, u32[]{:S(2)}, u32[]{:S(2)}) collective-permute-start(bf16[384,2,1280]{2,0,1:T(8,128)(2,1)} %pad_maximum_fusion.5), channel_id=1, source_target_pairs={{0,8},{8,0},{1,9},{9,1},{2,10},{10,2},{3,11},{11,3},{4,12},{12,4},... | collective-permute-start | bytes 5898248 | tf_op jit(solution)/shard_map/ppermute | solution.py:14
  372.5 3.5 copy-start.17
  377.9 4.4 copy-start.2
  377.9 26.7 %copy-start.7 = (bf16[192,2,1280]{0,2,1:T(8,128)(2,1)S(1)}, bf16[192,2,1280]{0,2,1:T(8,128)(2,1)}, u32[]{:S(2)}) copy-start(bf16[192,2,1280]{0,2,1:T(8,128)(2,1)} %copy-done.6) | copy-start | bytes 2949124
  407.4 1.1 copy-start.21
  415.5 32.7 %copy-start.9 = (bf16[96,2,1280]{0,2,1:T(8,128)(2,1)S(1)}, bf16[96,2,1280]{0,2,1:T(8,128)(2,1)}, u32[]{:S(2)}) copy-start(bf16[96,2,1280]{0,2,1:T(8,128)(2,1)} %copy-done.8) | copy-start | bytes 1474564
  451.7 1.0 copy-start.23
  469.1 4.1 copy-start.24
  473.2 1.5 copy-start.22
  478.0 7.8 %copy-start.10 = (f32[384,1280]{0,1:T(8,128)S(1)}, f32[384,1280]{0,1:T(8,128)}, u32[]{:S(2)}) copy-start(f32[384,1280]{0,1:T(8,128)} %copy.86) | copy-start | bytes 5898244
  478.0 7.8 %copy-start.11 = (f32[384,1280]{0,1:T(8,128)S(1)}, f32[384,1280]{0,1:T(8,128)}, u32[]{:S(2)}) copy-start(f32[384,1280]{0,1:T(8,128)} %copy.103) | copy-start | bytes 5898244
  478.0 7.8 %copy-start.12 = (f32[384,1280]{0,1:T(8,128)S(1)}, f32[384,1280]{0,1:T(8,128)}, u32[]{:S(2)}) copy-start(f32[384,1280]{0,1:T(8,128)} %copy.111) | copy-start | bytes 5898244
  486.9 7.0 %copy-start.1 = (bf16[1,384,2560]{2,1,0:T(8,128)(2,1)S(1)}, bf16[1,384,2560]{2,1,0:T(8,128)(2,1)}, u32[]{:S(2)}) copy-start(bf16[1,384,2560]{2,1,0:T(8,128)(2,1)} %param.4) | copy-start | bytes 5898244
Sparse Core Ops, SparseCore 0:
  9.0 237.9 all-gather.2
  248.6 86.8 all-gather.4
where the time goes:
time: 510 us; the launch traced here: 501 us
  waiting for transfers between devices  322 us (63%)
  local copies, waits for them, and re-layouts  65.4 us (13%)
  other arithmetic  51 us (10%)
  matrix products  35.1 us (7%)
  between operations  14.2 us (3%)
  starting transfers between devices  13.2 us (3%)
    all_gather x1, waiting for transfers between devices, local(): lax.all_gather(qkv_weight, 'dp', axis=1, tiled=True)  238 us
    ppermute x10, waiting for transfers between devices, from_partner(): return lax.ppermute(block, axis, route)  82.6 us
    concatenate x9, other arithmetic, local(): gathered = jnp.concatenate([gathered, partner], axis=0)  22.4 us
    reduce_sum x6, other arithmetic, select_rows(): jnp.sum(jnp.where(table, grouped, jnp.zeros((), grouped.dtype)), axis=1)  18.9 us
    ppermute x10, starting transfers between devices, from_partner(): return lax.ppermute(block, axis, route)  13.2 us
    dot_general x1, matrix products, local(): jnp.dot(token_flat, lax.all_gather(qkv_weight, 'dp', axis=1, tiled=True),...  12.3 us
    unnamed x65, local copies, waits for them, and re-layouts  12.3 us
    dot_general x4, matrix products, attend(): jnp.einsum('hqk,khd->qhd', expo.astype(jnp.bfloat16), value_rows, preferr...  11.6 us
  transfers between devices with their start and end apart: 12, of which 6 were waited for; matrix products, arithmetic and copies ran while one was open for 28% of the time, Pallas kernels for 0%

commit v1 on v0

--- a/solution.py
+++ b/solution.py
@@ -2,6 +2,13 @@
 import jax.numpy as jnp
 from jax import lax
 from jax.sharding import PartitionSpec as P
+
+
+def exchange_gather(x, mesh_axis, d):
+    size = lax.axis_size(mesh_axis)
+    blocks = jnp.stack([x for _ in range(size)])
+    blocks = lax.all_to_all(blocks, mesh_axis, split_axis=0, concat_axis=0)
+    return jnp.concatenate(blocks, axis=d)
 
 
 def from_partner(block, axis, stride):
@@ -48,9 +55,7 @@
     head_size = inner_width // head_count
     token_flat = tokens.reshape(tok_rows, tokens.shape[2])
     projected = jnp.dot(
-        token_flat,
-        lax.all_gather(qkv_weight, "dp", axis=1, tiled=True),
-        preferred_element_type=jnp.float32,
+        token_flat, exchange_gather(qkv_weight, "dp", 1), preferred_element_type=jnp.float32
     ).astype(jnp.bfloat16)
     all_query = projected[:, :inner_width].reshape(tok_rows, head_count, head_size)
     keyval = projected[:, inner_width:].reshape(tok_rows, 2, head_count, head_size)

time: 510 us -> 601 us (1.18)
  waiting for transfers between devices: 322 us -> 362 us
  local copies, waits for them, and re-layouts: 65.4 us -> 83.7 us
  other arithmetic: 51 us -> 67.6 us
  starting transfers between devices: 13.2 us -> 26.1 us
    all_to_all x0 -> x1, waiting for transfers between devices: none -> 281 us  [exchange_gather(): blocks = lax.all_to_all(blocks, mesh_axis, split_axis=0, concat_axis=0)]
    all_gather x1 -> x0, waiting for transfers between devices: 238 us -> none  [local(): lax.all_gather(qkv_weight, 'dp', axis=1, tiled=True)]
    another operation x0 -> x1, other arithmetic: none -> 16.9 us  [exchange_gather(): blocks = jnp.stack([x for _ in range(size)])]
    unnamed x65 -> x62, local copies, waits for them, and re-layouts: 12.3 us -> 25.1 us
    all_to_all x0 -> x1, starting transfers between devices: none -> 10.7 us  [exchange_gather(): blocks = lax.all_to_all(blocks, mesh_axis, split_axis=0, concat_axis=0)]
  transfers between devices with their start and end apart: 12 -> 12, of which waited for: 6 -> 6; matrix products, arithmetic and copies ran while one was open for 28% -> 25% of each run, Pallas kernels for 0% -> 0%
where the time goes in v1:
time: 601 us; the launch traced here: 591 us
  waiting for transfers between devices  362 us (60%)
  local copies, waits for them, and re-layouts  83.7 us (14%)
  other arithmetic  67.6 us (11%)
  matrix products  37.2 us (6%)
  starting transfers between devices  26.1 us (4%)
  between operations  14.4 us (2%)
    all_to_all x1, waiting for transfers between devices, exchange_gather(): blocks = lax.all_to_all(blocks, mesh_axis, split_axis=0, concat_axis=0)  281 us
    ppermute x10, waiting for transfers between devices, from_partner(): return lax.ppermute(block, axis, route)  80.2 us
    unnamed x62, local copies, waits for them, and re-layouts  25.1 us
    concatenate x9, other arithmetic, local(): gathered = jnp.concatenate([gathered, partner], axis=0)  22 us
    reduce_sum x6, other arithmetic, select_rows(): jnp.sum(jnp.where(table, grouped, jnp.zeros((), grouped.dtype)), axis=1)  19 us
    another operation x1, other arithmetic, exchange_gather(): blocks = jnp.stack([x for _ in range(size)])  16.9 us
    ppermute x10, starting transfers between devices, from_partner(): return lax.ppermute(block, axis, route)  15.4 us
    dot_general x1, matrix products, local(): jnp.dot(token_flat, exchange_gather(qkv_weight, 'dp', 1), preferred_eleme...  14.4 us
  transfers between devices with their start and end apart: 12, of which 6 were waited for; matrix products, arithmetic and copies ran while one was open for 25% of the time, Pallas kernels for 0%

profile of v1, /device:TPU:0, one launch (start us, length us, event | category | flops | bytes accessed | tf_op | source)
XLA Modules:
  0.0 591.2 jit_solution(15006677268361344178)
XLA Ops:
  6.5 13.7 %copy.76 = bf16[2560,1920]{0,1:T(8,128)(2,1)} copy(bf16[2560,1920]{1,0:T(8,128)(2,1)} %param.5) | data formatting | bytes 19660800 | tf_op args[1]
  20.3 16.9 %pad_maximum_fusion = bf16[2,2560,1920]{1,2,0:T(8,128)(2,1)} fusion(bf16[1,2560,1920]{1,2,0:T(8,128)(2,1)} %bitcast.149), kind=kLoop, calls=%fused_computation | loop fusion | flops 9830400 | bytes 29491200 | tf_op jit(solution)/shard_map/stack | solution.py:9
  37.2 10.7 %all-to-all-start = ((bf16[2,2560,1920]{1,2,0:T(8,128)(2,1)}), bf16[2,2560,1920]{1,2,0:T(8,128)(2,1)}, u32[]{:S(2)}, u32[]{:S(2)}) async-start(bf16[2,2560,1920]{1,2,0:T(8,128)(2,1)} %pad_maximum_fusion), calls=%async_computation | async-start | bytes 39321600 | tf_op jit(solution)/shard_map/all_to_all | solution.py:10
  50.1 281.4 %all-to-all-done = bf16[2,2560,1920]{1,2,0:T(8,128)(2,1)} async-done(((bf16[2,2560,1920]{1,2,0:T(8,128)(2,1)}), bf16[2,2560,1920]{1,2,0:T(8,128)(2,1)}, u32[]{:S(2)}, u32[]{:S(2)}) %all-to-all-start) | async-done | bytes 19660832 | tf_op jit(solution)/shard_map/all_to_all | solution.py:10
  331.4 14.4 %fusion.6 = bf16[384,3840]{0,1:T(8,128)(2,1)S(1)} fusion(bf16[2560,3840]{0,1:T(8,128)(2,1)} %bitcast.4, bf16[1,384,2560]{2,1,0:T(8,128)(2,1)S(1)} %copy-done), kind=kOutput, calls=%fused_computation.11 | convolution fusion | flops 7551221760 | bytes 24576000 | tf_op jit(solution)/shard_map/dot_general | solution.py:57
  345.9 1.5 slice.65
  347.3 1.1 slice.68
  348.5 2.7 copy.80
  351.2 2.7 reshape_reshape.27
  353.9 2.7 reshape_reshape.29
  356.6 4.9 select_reduce_fusion.1
  361.5 2.0 copy.81
  363.5 1.4 copy.82
  365.0 2.3 copy.79
  367.3 3.2 reshape_reshape.26
  370.5 3.3 select_reduce_fusion.4
  373.8 4.2 select_reduce_fusion
  378.0 2.6 copy.96
  380.6 2.1 copy.97
  383.2 2.1 select_reduce_fusion.2
  385.3 1.1 reshape.394
  387.1 3.2 broadcast_select_fusion
  390.4 1.6 fusion.42
  391.9 1.5 reshape_reshape.28
  394.8 2.1 collective-permute-start.7
  396.9 2.9 select_reduce_fusion.3
  399.9 1.4 copy.102
  401.2 1.6 pad_maximum_fusion.7
  402.9 2.3 copy.99
  405.2 4.0 collective-permute-done.7
  409.2 2.2 pad_maximum_fusion.8
  411.4 3.9 collective-permute-start.8
  416.8 1.5 copy.84
  418.4 2.0 pad_maximum_fusion.4
  420.4 1.1 collective-permute-start.2
  421.5 8.8 %collective-permute-done.4 = bf16[192,2,1280]{2,0,1:T(8,128)(2,1)} collective-permute-done((bf16[192,2,1280]{2,0,1:T(8,128)(2,1)}, bf16[192,2,1280]{2,0,1:T(8,128)(2,1)}, u32[]{:S(2)}, u32[]{:S(2)}) %collective-permute-start.4) | collective-permute-done | bytes 983072 | tf_op jit(solution)/shard_map/ppermute | solution.py:21
  430.4 1.5 copy.103
  431.9 3.5 pad_maximum_fusion.5
  435.5 3.9 collective-permute-start.5
  439.4 15.6 %collective-permute-done.8 = bf16[192,2,1280]{2,0,1:T(8,128)(2,1)} collective-permute-done((bf16[192,2,1280]{2,0,1:T(8,128)(2,1)}, bf16[192,2,1280]{2,0,1:T(8,128)(2,1)}, u32[]{:S(2)}, u32[]{:S(2)}) %collective-permute-start.8) | collective-permute-done | bytes 983072 | tf_op jit(solution)/shard_map/ppermute | solution.py:21
  455.0 2.7 pad_maximum_fusion.6
  457.7 3.2 collective-permute-start.9
  460.9 2.2 constant_dynamic-update-slice_fusion.1
  463.1 2.9 pad_maximum_fusion.3
  466.0 1.9 multiply_reduce_fusion
  468.0 2.7 fusion
  470.7 1.6 copy-done.2
  472.4 21.2 %collective-permute-done.2 = bf16[384,2,1280]{0,2,1:T(8,128)(2,1)} collective-permute-done((bf16[384,2,1280]{0,2,1:T(8,128)(2,1)}, bf16[384,2,1280]{0,2,1:T(8,128)(2,1)}, u32[]{:S(2)}, u32[]{:S(2)}) %collective-permute-start.2) | collective-permute-done | bytes 1966112 | tf_op jit(solution)/shard_map/ppermute | solution.py:21
  493.6 2.7 pad_maximum_fusion.1
  498.4 1.4 fusion.8
  499.7 1.6 fusion.46
  502.2 2.2 copy.151
  504.5 3.0 copy.93
  507.8 30.5 %collective-permute-done.5 = bf16[384,2,1280]{0,2,1:T(8,128)(2,1)} collective-permute-done((bf16[384,2,1280]{0,2,1:T(8,128)(2,1)}, bf16[384,2,1280]{0,2,1:T(8,128)(2,1)}, u32[]{:S(2)}, u32[]{:S(2)}) %collective-permute-start.5) | collective-permute-done | bytes 1966112 | tf_op jit(solution)/shard_map/ppermute | solution.py:21
  538.3 3.5 pad_maximum_fusion.2
  544.2 1.4 fusion.39
  547.0 1.8 copy.112
  549.1 3.0 constant_dynamic-update-slice_fusion
  552.0 4.3 fusion.68
  556.3 2.7 copy.116
  559.0 4.1 copy.119
  565.7 1.9 copy.122
  568.0 7.8 %fusion.22 = f32[384,10,128]{0,2,1:T(8,128)S(1)} fusion(bf16[768,10,128]{0,2,1:T(8,128)(2,1)} %bitcast.169, f32[10,384,768]{2,1,0:T(8,128)} %copy-done.2, f32[10,384]{1,0:T(8,128)S(1)} %get-tuple-element.25, f32[384,10]{0,1:T(8,128)S(1)} %get-tuple-element.11, f32[384,10]{0,1:T(8,128)S(1)} %bitcast.175, pred[10]{0:T(512)(128)(4,1)S(1)} %copy-done.24), kind=kOutput, calls=%fused_computation.48 | convolution fusion | flops 765296640 | bytes 15774730 | tf_op jit(solution)/shard_map/hqk,khd->qhd/dot_general | solution.py:44
  576.9 7.0 %fusion.9 = bf16[1,384,2560]{2,1,0:T(8,128)(2,1)} fusion(bf16[384,1280]{0,1:T(8,128)(2,1)S(1)} %fusion.17, bf16[1280,2560]{1,0:T(8,128)(2,1)} %all-gather.2.cloned.1.call-done), kind=kOutput, calls=%fused_computation.19 | convolution fusion | flops 2517565440 | bytes 9502720 | tf_op jit(solution)/shard_map/dot_general | solution.py:103
  (113 shorter events, 17.8 us)
Async XLA Ops:
  6.5 324.9 %copy-start = (bf16[1,384,2560]{2,1,0:T(8,128)(2,1)S(1)}, bf16[1,384,2560]{2,1,0:T(8,128)(2,1)}, u32[]{:S(2)}) copy-start(bf16[1,384,2560]{2,1,0:T(8,128)(2,1)} %param.4) | copy-start | bytes 5898244
  37.2 294.2 %all-to-all-start = ((bf16[2,2560,1920]{1,2,0:T(8,128)(2,1)}), bf16[2,2560,1920]{1,2,0:T(8,128)(2,1)}, u32[]{:S(2)}, u32[]{:S(2)}) async-start(bf16[2,2560,1920]{1,2,0:T(8,128)(2,1)} %pad_maximum_fusion), calls=%async_computation | async-start | bytes 39321600 | tf_op jit(solution)/shard_map/all_to_all | solution.py:10
  47.9 0.8 copy-start.27
  47.9 529.0 %all-gather.2.cloned.1.call-start = ((), (), s32[]{:S(2)}) async-start(), calls=%async_computation.1 | async-start | bytes 9830400 | tf_op jit(solution)/shard_map/all_gather | solution.py:105
  49.3 324.5 %copy-start.25 = (pred[4,10]{1,0:T(4,128)(4,1)}, pred[4,10]{1,0:T(4,128)(4,1)S(1)}, u32[]{:S(2)}) copy-start(pred[4,10]{1,0:T(4,128)(4,1)S(1)} %iota_compare_fusion.1) | copy-start | bytes 124
  49.5 0.5 copy-start.23
  364.9 52.0 %collective-permute-start.1 = (bf16[192,2,1280]{2,0,1:T(8,128)(2,1)}, bf16[192,2,1280]{2,0,1:T(8,128)(2,1)}, u32[]{:S(2)}, u32[]{:S(2)}) collective-permute-start(bf16[192,2,1280]{2,0,1:T(8,128)(2,1)} %copy.82), channel_id=1, source_target_pairs={{0,1},{1,0},{2,3},{3,2},{4,5},{5,4},{6,7},{7,6},{8,9},{9,8},{10,11... | collective-permute-start | bytes 2949128 | tf_op jit(solution)/shard_map/ppermute | solution.py:21
  382.7 17.2 %collective-permute-start.3 = (bf16[96,2,1280]{2,0,1:T(8,128)(2,1)}, bf16[96,2,1280]{2,0,1:T(8,128)(2,1)}, u32[]{:S(2)}, u32[]{:S(2)}) collective-permute-start(bf16[96,2,1280]{2,0,1:T(8,128)(2,1)} %copy.97), channel_id=1, source_target_pairs={{0,1},{1,0},{2,3},{3,2},{4,5},{5,4},{6,7},{7,6},{8,9},{9,8},{10,11... | collective-permute-start | bytes 1474568 | tf_op jit(solution)/shard_map/ppermute | solution.py:21
  387.1 6.8 %collective-permute-start.6 = (bf16[48,2,1280]{2,0,1:T(8,128)(2,1)S(1)}, bf16[48,2,1280]{2,0,1:T(8,128)(2,1)S(1)}, u32[]{:S(2)}, u32[]{:S(2)}) collective-permute-start(bf16[48,2,1280]{2,0,1:T(8,128)(2,1)S(1)} %get-tuple-element.20), channel_id=1, source_target_pairs={{0,1},{1,0},{2,3},{3,2},{4,5},{5,4},{6,7},{7,6},{8,9},{9,8},{10,11... | collective-permute-start | bytes 737288 | tf_op jit(solution)/shard_map/ppermute | solution.py:21
  387.1 3.2 copy-start.4
  391.9 5.0 copy-start.26
  393.4 7.8 %copy-start.3 = (bf16[96,2,10,128]{0,3,2,1:T(8,128)(2,1)S(1)}, bf16[96,2,10,128]{0,3,2,1:T(8,128)(2,1)}, u32[]{:S(2)}) copy-start(bf16[96,2,10,128]{0,3,2,1:T(8,128)(2,1)} %copy.96) | copy-start | bytes 1474564
  393.4 69.7 %collective-permute-start = (bf16[384,2,1280]{0,2,1:T(8,128)(2,1)}, bf16[384,2,1280]{0,2,1:T(8,128)(2,1)}, u32[]{:S(2)}, u32[]{:S(2)}) collective-permute-start(bf16[384,2,1280]{0,2,1:T(8,128)(2,1)} %broadcast_select_fusion), channel_id=1, source_target_pairs={{0,1},{1,0},{2,3},{3,2},{4,5},{5,4},{6,7},{7,6},{8,9},{9,8},{10,11... | collective-permute-start | bytes 5898248 | tf_op jit(solution)/shard_map/ppermute | solution.py:21
  393.9 5.9 %copy-start.16 = (bf16[48,2,1280]{2,0,1:T(8,128)(2,1)}, bf16[48,2,1280]{2,0,1:T(8,128)(2,1)S(1)}, u32[]{:S(2)}) copy-start(bf16[48,2,1280]{2,0,1:T(8,128)(2,1)S(1)} %collective-permute-done.6) | copy-start | bytes 737284
  394.8 14.4 %collective-permute-start.7 = (bf16[96,2,1280]{2,0,1:T(8,128)(2,1)}, bf16[96,2,1280]{2,0,1:T(8,128)(2,1)S(1)}, u32[]{:S(2)}, u32[]{:S(2)}) collective-permute-start(bf16[96,2,1280]{2,0,1:T(8,128)(2,1)} %pad_maximum_fusion.9), channel_id=1, source_target_pairs={{0,2},{2,0},{1,3},{3,1},{4,6},{6,4},{5,7},{7,5},{8,10},{10,8},{9,1... | collective-permute-start | bytes 1474568 | tf_op jit(solution)/shard_map/ppermute | solution.py:21
  401.2 4.0 copy-start.7
  405.2 10.1 %copy-start.17 = (bf16[48,2,1280]{2,0,1:T(8,128)(2,1)S(1)}, bf16[48,2,1280]{2,0,1:T(8,128)(2,1)}, u32[]{:S(2)}) copy-start(bf16[48,2,1280]{2,0,1:T(8,128)(2,1)} %copy-done.16) | copy-start | bytes 737284
  405.2 25.2 %collective-permute-start.4 = (bf16[192,2,1280]{2,0,1:T(8,128)(2,1)}, bf16[192,2,1280]{2,0,1:T(8,128)(2,1)}, u32[]{:S(2)}, u32[]{:S(2)}) collective-permute-start(bf16[192,2,1280]{2,0,1:T(8,128)(2,1)} %copy.99), channel_id=1, source_target_pairs={{0,2},{2,0},{1,3},{3,1},{4,6},{6,4},{5,7},{7,5},{8,10},{10,8},{9,1... | collective-permute-start | bytes 2949128 | tf_op jit(solution)/shard_map/ppermute | solution.py:21
  409.2 7.6 %copy-start.14 = (bf16[96,2,1280]{2,0,1:T(8,128)(2,1)}, bf16[96,2,1280]{2,0,1:T(8,128)(2,1)S(1)}, u32[]{:S(2)}) copy-start(bf16[96,2,1280]{2,0,1:T(8,128)(2,1)S(1)} %collective-permute-done.7) | copy-start | bytes 1474564
  411.4 43.6 %collective-permute-start.8 = (bf16[192,2,1280]{2,0,1:T(8,128)(2,1)}, bf16[192,2,1280]{2,0,1:T(8,128)(2,1)}, u32[]{:S(2)}, u32[]{:S(2)}) collective-permute-start(bf16[192,2,1280]{2,0,1:T(8,128)(2,1)} %pad_maximum_fusion.8), channel_id=1, source_target_pairs={{0,4},{4,0},{1,5},{5,1},{2,6},{6,2},{3,7},{7,3},{8,12},{12,8},{9,1... | collective-permute-start | bytes 2949128 | tf_op jit(solution)/shard_map/ppermute | solution.py:21
  418.4 2.0 copy-start.5
  420.4 73.1 %collective-permute-start.2 = (bf16[384,2,1280]{0,2,1:T(8,128)(2,1)}, bf16[384,2,1280]{0,2,1:T(8,128)(2,1)}, u32[]{:S(2)}, u32[]{:S(2)}) collective-permute-start(bf16[384,2,1280]{0,2,1:T(8,128)(2,1)} %pad_maximum_fusion.4), channel_id=1, source_target_pairs={{0,2},{2,0},{1,3},{3,1},{4,6},{6,4},{5,7},{7,5},{8,10},{10,8},{9,1... | collective-permute-start | bytes 5898248 | tf_op jit(solution)/shard_map/ppermute | solution.py:21
  431.9 23.1 %copy-start.15 = (bf16[96,2,1280]{2,0,1:T(8,128)(2,1)S(1)}, bf16[96,2,1280]{2,0,1:T(8,128)(2,1)}, u32[]{:S(2)}) copy-start(bf16[96,2,1280]{2,0,1:T(8,128)(2,1)} %copy-done.14) | copy-start | bytes 1474564
  431.9 23.1 %copy-start.18 = (bf16[48,2,1280]{2,0,1:T(8,128)(2,1)S(1)}, bf16[48,2,1280]{2,0,1:T(8,128)(2,1)}, u32[]{:S(2)}) copy-start(bf16[48,2,1280]{2,0,1:T(8,128)(2,1)} %copy-done.16) | copy-start | bytes 737284
  435.5 102.8 %collective-permute-start.5 = (bf16[384,2,1280]{0,2,1:T(8,128)(2,1)}, bf16[384,2,1280]{0,2,1:T(8,128)(2,1)}, u32[]{:S(2)}, u32[]{:S(2)}) collective-permute-start(bf16[384,2,1280]{0,2,1:T(8,128)(2,1)} %pad_maximum_fusion.5), channel_id=1, source_target_pairs={{0,4},{4,0},{1,5},{5,1},{2,6},{6,2},{3,7},{7,3},{8,12},{12,8},{9,1... | collective-permute-start | bytes 5898248 | tf_op jit(solution)/shard_map/ppermute | solution.py:21
  457.7 5.4 copy-start.13
  457.7 91.4 %collective-permute-start.9 = (bf16[384,2,1280]{2,0,1:T(8,128)(2,1)}, bf16[384,2,1280]{2,0,1:T(8,128)(2,1)}, u32[]{:S(2)}, u32[]{:S(2)}) collective-permute-start(bf16[384,2,1280]{2,0,1:T(8,128)(2,1)} %pad_maximum_fusion.6), channel_id=1, source_target_pairs={{0,8},{8,0},{1,9},{9,1},{2,10},{10,2},{3,11},{11,3},{4,12},{12,4},... | collective-permute-start | bytes 5898248 | tf_op jit(solution)/shard_map/ppermute | solution.py:21
  463.1 2.9 copy-start.9
  463.1 2.9 copy-start.24
  468.0 4.4 copy-start.2
  468.0 25.6 %copy-start.6 = (bf16[192,2,1280]{0,2,1:T(8,128)(2,1)S(1)}, bf16[192,2,1280]{0,2,1:T(8,128)(2,1)}, u32[]{:S(2)}) copy-start(bf16[192,2,1280]{0,2,1:T(8,128)(2,1)} %copy-done.5) | copy-start | bytes 2949124
  496.2 1.1 copy-start.19
  504.5 33.8 %copy-start.8 = (bf16[96,2,1280]{0,2,1:T(8,128)(2,1)S(1)}, bf16[96,2,1280]{0,2,1:T(8,128)(2,1)}, u32[]{:S(2)}) copy-start(bf16[96,2,1280]{0,2,1:T(8,128)(2,1)} %copy-done.7) | copy-start | bytes 1474564
  541.8 1.0 copy-start.21
  559.0 4.1 copy-start.22
  563.1 1.5 copy-start.20
  568.0 7.8 %copy-start.10 = (f32[384,1280]{0,1:T(8,128)S(1)}, f32[384,1280]{0,1:T(8,128)}, u32[]{:S(2)}) copy-start(f32[384,1280]{0,1:T(8,128)} %copy.93) | copy-start | bytes 5898244
  568.0 7.8 %copy-start.11 = (f32[384,1280]{0,1:T(8,128)S(1)}, f32[384,1280]{0,1:T(8,128)}, u32[]{:S(2)}) copy-start(f32[384,1280]{0,1:T(8,128)} %copy.112) | copy-start | bytes 5898244
  568.0 7.8 %copy-start.12 = (f32[384,1280]{0,1:T(8,128)S(1)}, f32[384,1280]{0,1:T(8,128)}, u32[]{:S(2)}) copy-start(f32[384,1280]{0,1:T(8,128)} %copy.122) | copy-start | bytes 5898244
  576.9 7.0 %copy-start.1 = (bf16[1,384,2560]{2,1,0:T(8,128)(2,1)S(1)}, bf16[1,384,2560]{2,1,0:T(8,128)(2,1)}, u32[]{:S(2)}) copy-start(bf16[1,384,2560]{2,1,0:T(8,128)(2,1)} %param.4) | copy-start | bytes 5898244
Sparse Core Ops, SparseCore 0:
  50.4 159.1 all-gather.1
